TPU v7x, 256 devices: a whole 4x4x8 slice. The times are simulated.
256 devices in a mesh: ctx: 32 (over z_lo, x, core), wt: 8 (over y, z_hi).
Axes of the slice: x: 4, y: 4, z: 8 (z_hi: 2, z_lo: 4; z = z_hi * 4 + z_lo), core: 2. Of those that a mesh axis runs over, the one named last changes fastest.
Arguments:
- patches: bfloat16 [16384, 1280], P('ctx'), may hold values from -6 to 6
- vit_gain: float32 [1280], replicated, may hold values from 0.5 to 1.5
- vit_codes: bfloat16 [1280, 3, 1280], P(None, None, 'wt'), may hold values from -1 to 1
- vit_scales: bfloat16 [8], P('wt'), may hold values from 0.5 to 2
- vit_bias: float32 [3, 1280], P(None, 'wt'), may hold values from -3 to 3
- window_ids: int32 [16384], P('ctx'), may hold values from 63 to 16383, as said below
- merger_codes: bfloat16 [4, 1280, 8192], P(None, 'wt', 'ctx'), may hold values from -0.078125 to 0.078125
- merger_scales: bfloat16 [1, 8, 8192], P(None, 'wt', 'ctx'), may hold values from 0.5 to 2
- merger_bias: float32 [8192], P('wt'), may hold values from -3 to 3
- positions: int32 [4096], P('ctx'), may hold values from 0 to 16383, as said below
- text_embed: bfloat16 [16384, 8192], P('ctx', 'wt'), may hold values from -6 to 6
- norm_gain: float32 [8192], P('wt'), may hold values from 0.5 to 1.5
- llm_codes: bfloat16 [8192, 8, 768], P('wt', None, 'ctx'), may hold values from -1 to 1
- llm_scales: bfloat16 [8, 8, 768], P('wt', None, 'ctx'), may hold values from 0.5 to 2
- llm_bias: float32 [8, 768], P('wt'), may hold values from -3 to 3
- segments: int32 [16384], P('ctx'), may hold values from 0 to 15, never falling along the last dimension, each value on 1 to 2048 neighbouring positions
Outputs:
- attention_out: bfloat16 [16384, 4096], P('ctx', 'wt')
Inputs may be any that keep to these rules, and one draw needn't show every extreme that they name: `window_ids`: windows are runs of consecutive patches of at most 64, never crossing a block of 512 patches; patches of one window share the id, different windows have different ids. `positions`: distinct. The 128 entries of one aligned block (one device's merged tokens) put at most 8 into any one block of 512 positions, and exactly 8 into some block. `segments`: never falling; each run of equal ids is at most 2048 positions long.
All inputs are finite; a program needn't handle non-finite values.
Results may differ from a plain program's by a relative error of at most 0.025.
Values may be sent and summed in bfloat16 or wider, within the bound.
A program may use at most 128 MiB of HBM per device.

v0:
```python
import jax
import jax.numpy as jnp
from jax import lax
from jax.sharding import PartitionSpec as P

VHD = 80
D = 8192
KVH = 8
HD = 128
GROUP = 4
MERGE = 4
REACH = 4
VIT_EPS = 1e-06
RMS_EPS = 1e-06
ROPE_BASE = 1000000.0
FILL_LOW = -1e30


def in_blocks(x, dim, peers):
    before, after = (x.shape[:dim], x.shape[dim + 1 :])
    return jnp.moveaxis(x.reshape(*before, peers, -1, *after), dim, 0)


def summed_on_arrival(x, axis, dim):
    parts = in_blocks(x, dim, lax.axis_size(axis))
    arrived = lax.all_to_all(parts, axis, split_axis=0, concat_axis=0, tiled=True)
    return arrived.astype(jnp.float32).sum(axis=0)


def passed_along(value, axis, steps):
    count = lax.axis_size(axis)
    leading, last = (max(0, -steps), min(count, count - steps))
    return lax.ppermute(value, axis, [(source, source + steps) for source in range(leading, last)])


def softmax_rows(scores, allowed):
    masked = jnp.where(allowed, scores, FILL_LOW)
    highest = jnp.max(masked, axis=-1, keepdims=True)
    raised = jnp.exp(masked - highest)
    return raised / jnp.sum(raised, axis=-1, keepdims=True)


def vision_norm_rows(patches, vit_gain):
    values = patches.astype(jnp.float32)
    mean_square = jnp.mean(values * values, axis=1, keepdims=True)
    return (values * lax.rsqrt(mean_square + VIT_EPS) * vit_gain).astype(jnp.bfloat16)


def window_attention(normed, weight_block, bias_block, window_ids):
    row_count = normed.shape[0]
    packed = jnp.dot(
        normed, weight_block.reshape(normed.shape[1], -1), preferred_element_type=jnp.float32
    )
    triple = (packed.reshape(row_count, 3, -1) + bias_block).astype(jnp.bfloat16)
    heads_here = triple.shape[2] // VHD
    queries = triple[:, 0].reshape(row_count, heads_here, VHD)
    keys_here = triple[:, 1].reshape(row_count, heads_here, VHD)
    values_here = triple[:, 2].reshape(row_count, heads_here, VHD)
    scores = jnp.einsum(
        "qhd,khd->hqk", queries, keys_here, preferred_element_type=jnp.float32
    ) * VHD ** (-0.5)
    allowed = window_ids[:, None] == window_ids[None, :]
    softmaxed = softmax_rows(scores, allowed[None]).astype(jnp.bfloat16)
    blended = jnp.einsum("hqk,khd->qhd", softmaxed, values_here, preferred_element_type=jnp.float32)
    return blended.astype(jnp.bfloat16).reshape(row_count, -1)


def rope_tables(first, length):
    places = (first + jnp.arange(length, dtype=jnp.int32)).astype(jnp.float32)
    frequency = ROPE_BASE ** (-jnp.arange(0, HD, 2).astype(jnp.float32) / HD)
    angles = places[:, None] * frequency[None, :]
    angles = jnp.concatenate([angles, angles], axis=1)
    return (jnp.cos(angles), jnp.sin(angles))


def rotary(inputs, cosine, sine):
    halfway = inputs.shape[-1] // 2
    turned = jnp.concatenate([-inputs[..., halfway:], inputs[..., :halfway]], axis=-1)
    return inputs * cosine + turned * sine


def split_heads(triple, cosine, sine):
    row_count, group_count = (triple.shape[0], triple.shape[1])
    queries = triple[:, :, : GROUP * HD].reshape(row_count, group_count, GROUP, HD)
    queries = rotary(queries, cosine[:, None, None, :], sine[:, None, None, :]).astype(jnp.bfloat16)
    keys_rot = rotary(
        triple[:, :, GROUP * HD : (GROUP + 1) * HD], cosine[:, None, :], sine[:, None, :]
    ).astype(jnp.bfloat16)
    values_cut = triple[:, :, (GROUP + 1) * HD :].astype(jnp.bfloat16)
    return (queries, keys_rot, values_cut)


def merge_project(features, merger_codes, merger_scales, merger_bias):
    row_count = features.shape[0]
    flat = features.reshape(row_count, -1)
    codes_piece = lax.all_gather(merger_codes, "ctx", axis=2, tiled=True)
    scale_piece = lax.all_gather(merger_scales, "ctx", axis=2, tiled=True)
    width = codes_piece.shape[2]
    dequant = (codes_piece.astype(jnp.float32) * scale_piece.astype(jnp.float32)).astype(
        jnp.bfloat16
    )
    product = jnp.dot(flat, dequant.reshape(-1, width), preferred_element_type=jnp.float32)
    mine = summed_on_arrival(product.astype(jnp.bfloat16), "wt", 1)
    return (mine + merger_bias).astype(jnp.bfloat16)


def route_tokens(values, positions, span):
    owners = lax.axis_size("ctx")
    items = values.shape[0]
    capacity = 2 * positions.shape[0] // owners
    target = positions // span
    item_order = jnp.arange(items, dtype=jnp.int32)
    before = (target[None, :] == target[:, None]) & (item_order[None, :] < item_order[:, None])
    ranks = jnp.sum(before.astype(jnp.int32), axis=1)
    slots = target * capacity + ranks
    table = slots[None, :] == jnp.arange(owners * capacity, dtype=jnp.int32)[:, None]
    packed = jnp.dot(table.astype(jnp.bfloat16), values, preferred_element_type=jnp.float32).astype(
        jnp.bfloat16
    )
    labels = jnp.sum(jnp.where(table, positions[None, :] + 1, 0), axis=1) - 1
    return (
        lax.all_to_all(packed, "ctx", split_axis=0, concat_axis=0, tiled=True),
        lax.all_to_all(labels, "ctx", split_axis=0, concat_axis=0, tiled=True),
    )


def place_tokens(text_embed, arrived, labels, first):
    local = labels - first
    table = local[None, :] == jnp.arange(text_embed.shape[0], dtype=jnp.int32)[:, None]
    filled = jnp.dot(
        table.astype(jnp.bfloat16), arrived, preferred_element_type=jnp.float32
    ).astype(jnp.bfloat16)
    covered = jnp.any(table, axis=1)
    return jnp.where(covered[:, None], filled, text_embed)


def on_device(
    patches,
    vit_gain,
    vit_codes,
    vit_scales,
    vit_bias,
    window_ids,
    merger_codes,
    merger_scales,
    merger_bias,
    positions,
    text_embed,
    norm_gain,
    llm_codes,
    llm_scales,
    llm_bias,
    segments,
):
    early_codes, early_scales = (
        lax.all_gather(llm_codes, "ctx", axis=2, tiled=True),
        lax.all_gather(llm_scales, "ctx", axis=2, tiled=True),
    )
    row_count = text_embed.shape[0]
    first = lax.axis_index("ctx") * row_count
    normed_patches = vision_norm_rows(patches, vit_gain)
    vit_weight = (vit_codes.astype(jnp.float32) * vit_scales.astype(jnp.float32)[0]).astype(
        jnp.bfloat16
    )
    attended = window_attention(normed_patches, vit_weight, vit_bias, window_ids)
    token_count = positions.shape[0]
    features = attended.reshape(token_count, MERGE, -1)
    projected = merge_project(features, merger_codes, merger_scales, merger_bias)
    embedded, labels = route_tokens(projected, positions, row_count)
    hidden = place_tokens(text_embed, embedded, labels, first)
    values = hidden.astype(jnp.float32)
    squares = lax.psum(jnp.sum(values * values, axis=1), "wt")
    normed = (values * lax.rsqrt(squares[:, None] / D + RMS_EPS) * norm_gain).astype(jnp.bfloat16)
    local_rows = normed.shape[1]
    dequant = (early_codes.astype(jnp.float32) * early_scales.astype(jnp.float32)).astype(
        jnp.bfloat16
    )
    partial_value = jnp.dot(
        normed, dequant.reshape(local_rows, -1), preferred_element_type=jnp.float32
    ).reshape(row_count, KVH, -1)
    triple = (
        lax.psum_scatter(
            partial_value.astype(jnp.bfloat16), "wt", scatter_dimension=1, tiled=True
        ).astype(jnp.float32)
        + llm_bias
    )
    cosine, sine = rope_tables(first, row_count)
    queries, keys_rot, values_cut = split_heads(triple, cosine, sine)
    own = (keys_rot, values_cut, segments)
    arrivals = [own]
    for distance in range(1, REACH + 1):
        arrivals.append(passed_along((own[0], own[1], own[2]), "ctx", distance))
    keys_all = jnp.concatenate([arrival[0] for arrival in arrivals], axis=0)
    values_all = jnp.concatenate([arrival[1] for arrival in arrivals], axis=0)
    key_segments = jnp.concatenate([arrival[2] for arrival in arrivals], axis=0)
    key_places = jnp.concatenate(
        [
            first - distance * row_count + jnp.arange(row_count, dtype=jnp.int32)
            for distance in range(REACH + 1)
        ],
        axis=0,
    )
    query_places = first + jnp.arange(row_count, dtype=jnp.int32)
    allowed = (
        (segments[:, None] == key_segments[None, :])
        & (key_places[None, :] <= query_places[:, None])
        & (key_places[None, :] >= 0)
    )
    scores = jnp.einsum(
        "qjd,kd->jqk", queries[:, 0], keys_all[:, 0], preferred_element_type=jnp.float32
    ) * HD ** (-0.5)
    softmaxed = softmax_rows(scores, allowed[None]).astype(jnp.bfloat16)
    blended = jnp.einsum(
        "jqk,kd->qjd", softmaxed, values_all[:, 0], preferred_element_type=jnp.float32
    )
    outputs = blended.astype(jnp.bfloat16).reshape(row_count, -1)
    return outputs


def solution(mesh):
    in_specs = (
        P("ctx", None),
        P(),
        P(None, None, "wt"),
        P("wt"),
        P(None, "wt"),
        P("ctx"),
        P(None, "wt", "ctx"),
        P(None, "wt", "ctx"),
        P("wt"),
        P("ctx"),
        P("ctx", "wt"),
        P("wt"),
        P("wt", None, "ctx"),
        P("wt", None, "ctx"),
        P("wt", None),
        P("ctx"),
    )
    out_specs = P("ctx", "wt")
    return jax.shard_map(
        on_device, mesh=mesh, in_specs=in_specs, out_specs=out_specs, check_vma=False
    )
```

profile of v0, /device:TPU:1, one launch (start us, length us, event | category | flops | bytes accessed | tf_op | source)
XLA Modules:
  0.0 532.9 jit_solution(2838187777075380373)
XLA Ops:
  16.2 45.9 %all_gather.13 = bf16[1,1,8192]{2,1,0:T(2,128)(2,1)S(1)} all-gather(bf16[1,1,256]{2,1,0:T(2,128)(2,1)S(1)} %copy-done.8), channel_id=1, replica_groups=mesh['ctx'=32,'wt'=8] {'ctx'}, dimensions={2}, use_global_device_ids=true | all-gather | bytes 16896 | tf_op jit(solution)/shard_map/all_gather | solution.py:97
  62.2 47.2 %all-gather.3.cloned.1.call-done = bf16[4,160,8192]{2,1,0:T(8,128)(2,1)} async-done(((bf16[4,160,256]{2,1,0:T(8,128)(2,1)}), bf16[4,160,8192]{2,1,0:T(8,128)(2,1)}) %all-gather.3.cloned.1.call-update) | async-done | bytes 10485776 | tf_op jit(solution)/shard_map/all_gather | solution.py:96
  109.4 6.2 %multiply_convert_fusion.1 = bf16[4,160,8192]{2,1,0:T(8,128)(2,1)S(1)} fusion(bf16[4,160,8192]{2,1,0:T(8,128)(2,1)} %all-gather.3.cloned.1.call-done, f32[8192]{0:T(1024)S(1)} %bitcast.110), kind=kLoop, calls=%fused_computation.6 | loop fusion | flops 15728640 | bytes 21004288 | tf_op jit(solution)/shard_map/convert_element_type | solution.py:99
  119.1 7.4 %all-to-all-start.1 = ((bf16[8,128,1024]{2,1,0:T(8,128)(2,1)}), bf16[8,128,1024]{2,1,0:T(8,128)(2,1)S(1)}, u32[]{:S(2)}, u32[]{:S(2)}) async-start(bf16[8,128,1024]{2,1,0:T(8,128)(2,1)} %bitcast.102), calls=%async_computation.1 | async-start | bytes 4194304 | tf_op jit(solution)/shard_map/all_to_all | solution.py:26
  127.6 74.6 %all-to-all-done.1 = bf16[8,128,1024]{2,1,0:T(8,128)(2,1)S(1)} async-done(((bf16[8,128,1024]{2,1,0:T(8,128)(2,1)}), bf16[8,128,1024]{2,1,0:T(8,128)(2,1)S(1)}, u32[]{:S(2)}, u32[]{:S(2)}) %all-to-all-start.1) | async-done | bytes 2097184 | tf_op jit(solution)/shard_map/all_to_all | solution.py:26
  202.2 4.9 all-to-all-start
  208.6 6.0 %all-to-all-done = s32[32,8,1]{1,2,0:T(1,128)S(1)} async-done(((s32[32,8,1]{1,2,0:T(1,128)}), s32[32,8,1]{1,2,0:T(1,128)S(1)}, u32[]{:S(2)}, u32[]{:S(2)}) %all-to-all-start) | async-done | bytes 1056 | tf_op jit(solution)/shard_map/all_to_all | solution.py:123
  214.6 4.1 all-to-all-start.2
  218.9 54.9 %all_gather.15 = bf16[1,8,768]{1,0,2:T(2,128)(2,1)S(1)} all-gather(bf16[1,8,24]{1,0,2:T(2,128)(2,1)S(1)} %copy.42), channel_id=1, replica_groups=mesh['ctx'=32,'wt'=8] {'ctx'}, dimensions={2}, use_global_device_ids=true | all-gather | bytes 12672 | tf_op jit(solution)/shard_map/all_gather | solution.py:157
  275.3 22.5 %psum.7 = f32[512]{0:T(512)S(1)} all-reduce(f32[512]{0:T(512)S(1)} %get-tuple-element.24), channel_id=1, replica_groups=mesh['ctx'=32,'wt'=8] {'wt'}, use_global_device_ids=true, to_apply=%region_8.9 | all-reduce | flops 512 | bytes 4096 | tf_op jit(solution)/shard_map/psum | solution.py:172
  297.8 11.6 %fusion.11 = bf16[512,8,768]{2,0,1:T(8,128)(2,1)} fusion(bf16[1024,8,768]{0,2,1:T(8,128)(2,1)} %all-gather.5.cloned.1.call-done, f32[8,768]{1,0:T(8,128)S(1)} %copy.43, bf16[512,1024]{1,0:T(8,128)(2,1)S(1)} %get-tuple-element.25, f32[1024]{0:T(1024)S(1)} %copy-done.12, f32[512]{0:T(512)S(1)} %add_rsqrt_fusion), kind=kOutput, calls=%fused_computation.18 | convolution fusion | flops 6466568192 | bytes 19953664 | tf_op jit(solution)/shard_map/dot_general | solution.py:178
  310.1 4.9 collective-permute-start.4
  322.3 3.5 and_and_fusion
  325.8 132.5 %reduce-scatter.2.cloned.1.call-done = bf16[512,1,768]{2,0,1:T(8,128)(2,1)} async-done(((bf16[512,8,768]{2,0,1:T(8,128)(2,1)}), bf16[512,1,768]{2,0,1:T(8,128)(2,1)}) %reduce-scatter.2.cloned.1.call-update) | async-done | bytes 786448 | tf_op jit(solution)/shard_map/reduce_scatter | solution.py:182
  461.6 5.8 %collective-permute-start = (bf16[512,1,128]{2,0,1:T(8,128)(2,1)}, bf16[512,1,128]{2,0,1:T(8,128)(2,1)S(1)}, u32[]{:S(2)}, u32[]{:S(2)}) collective-permute-start(bf16[512,1,128]{2,0,1:T(8,128)(2,1)} %get-tuple-element.6), channel_id=1, source_target_pairs={{0,8},{8,16},{16,24},{24,32},{32,40},{40,48},{48,56},{56,64},{64,7... | collective-permute-start | bytes 393224 | tf_op jit(solution)/shard_map/ppermute | solution.py:33
  467.3 3.1 collective-permute-start.1
  470.4 3.4 collective-permute-start.2
  475.0 2.5 collective-permute-start.8
  477.5 3.8 collective-permute-start.9
  485.2 2.6 mul.223
  489.4 3.3 collective-permute-start.10
  498.2 4.5 collective-permute-start.3
  504.1 12.6 %fusion.83 = (f32[4,512]{1,0:T(4,128)S(1)}, f32[4,512,2560]{1,2,0:T(8,128)}) fusion(pred[512,2560]{0,1:T(8,128)(4,1)S(1)} %copy-done.2, bf16[2560,1,128]{2,0,1:T(8,128)(2,1)} %constant_dynamic-update-slice_fusion.7, bf16[512,4,128]{2,1,0:T(4,128)(2,1)S(1)} %convert_element_type.133), kind=kOutput, calls=%fused_computation.137 | convolution fusion | flops 1363151360 | bytes 23470080 | tf_op jit(solution)/shard_map/sub | solution.py:39
  516.9 8.5 %fusion.28 = bf16[128,4,512]{2,0,1:T(8,128)(2,1)S(1)} fusion(f32[4,512,2560]{1,2,0:T(8,128)} %get-tuple-element.27, f32[4,512]{1,0:T(4,128)S(1)} %get-tuple-element.26, bf16[2560,1,128]{2,0,1:T(8,128)(2,1)S(1)} %constant_dynamic-update-slice_fusion), kind=kOutput, calls=%fused_computation.44 | convolution fusion | flops 1352925184 | bytes 22159360 | tf_op jit(solution)/shard_map/jqk,kd->qjd/dot_general | solution.py:213
  (118 shorter events, 42.1 us)
Async XLA Ops:
  6.5 102.9 %all-gather.3.cloned.1.call-start = ((), (), s32[]{:S(2)}) async-start(), calls=%async_computation.4 | async-start | bytes 10813440 | tf_op jit(solution)/shard_map/all_gather | solution.py:96
  7.3 290.5 %all-gather.5.cloned.1.call-start = ((), (), s32[]{:S(2)}) async-start(), calls=%async_computation.5 | async-start | bytes 12976128 | tf_op jit(solution)/shard_map/all_gather | solution.py:156
  119.1 83.1 %all-to-all-start.1 = ((bf16[8,128,1024]{2,1,0:T(8,128)(2,1)}), bf16[8,128,1024]{2,1,0:T(8,128)(2,1)S(1)}, u32[]{:S(2)}, u32[]{:S(2)}) async-start(bf16[8,128,1024]{2,1,0:T(8,128)(2,1)} %bitcast.102), calls=%async_computation.1 | async-start | bytes 4194304 | tf_op jit(solution)/shard_map/all_to_all | solution.py:26
  126.5 81.0 %copy-start.5 = (f32[1024]{0:T(1024)S(1)}, f32[1024]{0:T(1024)}, u32[]{:S(2)}) copy-start(f32[1024]{0:T(1024)} %param.24) | copy-start | bytes 12292
  202.2 12.4 %all-to-all-start = ((s32[32,8,1]{1,2,0:T(1,128)}), s32[32,8,1]{1,2,0:T(1,128)S(1)}, u32[]{:S(2)}, u32[]{:S(2)}) async-start(s32[32,8,1]{1,2,0:T(1,128)} %bitcast), calls=%async_computation | async-start | bytes 32768 | tf_op jit(solution)/shard_map/all_to_all | solution.py:123
  207.1 11.6 %copy-start.7 = (bf16[1,8,24]{2,1,0:T(8,128)(2,1)S(1)}, bf16[1,8,24]{2,1,0:T(8,128)(2,1)}, u32[]{:S(2)}) copy-start(bf16[1,8,24]{2,1,0:T(8,128)(2,1)} %param.29) | copy-start | bytes 1156
  207.5 67.2 %copy-start.9 = (bf16[512,1024]{1,0:T(8,128)(2,1)S(1)}, bf16[512,1024]{1,0:T(8,128)(2,1)}, u32[]{:S(2)}) copy-start(bf16[512,1024]{1,0:T(8,128)(2,1)} %param.26) | copy-start | bytes 3145732
  214.6 60.0 %all-to-all-start.2 = ((bf16[32,8,1024]{2,1,0:T(8,128)(2,1)}), bf16[32,8,1024]{2,1,0:T(8,128)(2,1)S(1)}, u32[]{:S(2)}, u32[]{:S(2)}) async-start(bf16[32,8,1024]{2,1,0:T(8,128)(2,1)} %fusion.32), calls=%async_computation.2 | async-start | bytes 1048576 | tf_op jit(solution)/shard_map/all_to_all | solution.py:122
  218.7 239.6 %reduce-scatter.2.cloned.1.call-start = ((), (), s32[]{:S(2)}) async-start(), calls=%async_computation.6 | async-start | bytes 7077888 | tf_op jit(solution)/shard_map/reduce_scatter | solution.py:182
  274.2 23.6 %copy-start.12 = (f32[1024]{0:T(1024)S(1)}, f32[1024]{0:T(1024)}, u32[]{:S(2)}) copy-start(f32[1024]{0:T(1024)} %param.27) | copy-start | bytes 12292
  310.1 12.1 %collective-permute-start.4 = (s32[512]{0:T(512)S(1)}, s32[512]{0:T(512)S(1)}, u32[]{:S(2)}, u32[]{:S(2)}) collective-permute-start(s32[512]{0:T(512)S(1)} %copy-done.4), channel_id=1, source_target_pairs={{0,8},{8,16},{16,24},{24,32},{32,40},{40,48},{48,56},{56,64},{64,7... | collective-permute-start | bytes 6152 | tf_op jit(solution)/shard_map/ppermute | solution.py:33
  315.0 7.3 %collective-permute-start.5 = (s32[512]{0:T(512)S(1)}, s32[512]{0:T(512)S(1)}, u32[]{:S(2)}, u32[]{:S(2)}) collective-permute-start(s32[512]{0:T(512)S(1)} %copy-done.4), channel_id=1, source_target_pairs={{0,16},{8,24},{16,32},{24,40},{32,48},{40,56},{48,64},{56,72},{64,... | collective-permute-start | bytes 6152 | tf_op jit(solution)/shard_map/ppermute | solution.py:33
  316.3 6.0 %collective-permute-start.6 = (s32[512]{0:T(512)S(1)}, s32[512]{0:T(512)S(1)}, u32[]{:S(2)}, u32[]{:S(2)}) collective-permute-start(s32[512]{0:T(512)S(1)} %copy-done.4), channel_id=1, source_target_pairs={{0,24},{8,32},{16,40},{24,48},{32,56},{40,64},{48,72},{56,80},{64,... | collective-permute-start | bytes 6152 | tf_op jit(solution)/shard_map/ppermute | solution.py:33
  317.6 4.7 collective-permute-start.7
  461.6 55.2 %collective-permute-start = (bf16[512,1,128]{2,0,1:T(8,128)(2,1)}, bf16[512,1,128]{2,0,1:T(8,128)(2,1)S(1)}, u32[]{:S(2)}, u32[]{:S(2)}) collective-permute-start(bf16[512,1,128]{2,0,1:T(8,128)(2,1)} %get-tuple-element.6), channel_id=1, source_target_pairs={{0,8},{8,16},{16,24},{24,32},{32,40},{40,48},{48,56},{56,64},{64,7... | collective-permute-start | bytes 393224 | tf_op jit(solution)/shard_map/ppermute | solution.py:33
  467.3 49.4 %collective-permute-start.1 = (bf16[512,1,128]{2,0,1:T(8,128)(2,1)}, bf16[512,1,128]{2,0,1:T(8,128)(2,1)S(1)}, u32[]{:S(2)}, u32[]{:S(2)}) collective-permute-start(bf16[512,1,128]{2,0,1:T(8,128)(2,1)} %get-tuple-element.6), channel_id=1, source_target_pairs={{0,16},{8,24},{16,32},{24,40},{32,48},{40,56},{48,64},{56,72},{64,... | collective-permute-start | bytes 393224 | tf_op jit(solution)/shard_map/ppermute | solution.py:33
  470.4 46.3 %collective-permute-start.2 = (bf16[512,1,128]{2,0,1:T(8,128)(2,1)}, bf16[512,1,128]{2,0,1:T(8,128)(2,1)S(1)}, u32[]{:S(2)}, u32[]{:S(2)}) collective-permute-start(bf16[512,1,128]{2,0,1:T(8,128)(2,1)} %get-tuple-element.6), channel_id=1, source_target_pairs={{0,24},{8,32},{16,40},{24,48},{32,56},{40,64},{48,72},{56,80},{64,... | collective-permute-start | bytes 393224 | tf_op jit(solution)/shard_map/ppermute | solution.py:33
  475.0 14.3 %collective-permute-start.8 = (bf16[512,1,128]{2,0,1:T(8,128)(2,1)}, bf16[512,1,128]{2,0,1:T(8,128)(2,1)}, u32[]{:S(2)}, u32[]{:S(2)}) collective-permute-start(bf16[512,1,128]{2,0,1:T(8,128)(2,1)} %get-tuple-element.10), channel_id=1, source_target_pairs={{0,8},{8,16},{16,24},{24,32},{32,40},{40,48},{48,56},{56,64},{64,7... | collective-permute-start | bytes 393224 | tf_op jit(solution)/shard_map/ppermute | solution.py:33
  477.5 16.7 %collective-permute-start.9 = (bf16[512,1,128]{2,0,1:T(8,128)(2,1)}, bf16[512,1,128]{2,0,1:T(8,128)(2,1)}, u32[]{:S(2)}, u32[]{:S(2)}) collective-permute-start(bf16[512,1,128]{2,0,1:T(8,128)(2,1)} %get-tuple-element.10), channel_id=1, source_target_pairs={{0,16},{8,24},{16,32},{24,40},{32,48},{40,56},{48,64},{56,72},{64,... | collective-permute-start | bytes 393224 | tf_op jit(solution)/shard_map/ppermute | solution.py:33
  489.2 14.9 %copy-start.2 = (pred[512,2560]{0,1:T(8,128)(4,1)S(1)}, pred[512,2560]{0,1:T(8,128)(4,1)}, u32[]{:S(2)}) copy-start(pred[512,2560]{0,1:T(8,128)(4,1)} %and_and_fusion) | copy-start | bytes 3932164
  489.4 8.8 %collective-permute-start.10 = (bf16[512,1,128]{2,0,1:T(8,128)(2,1)}, bf16[512,1,128]{2,0,1:T(8,128)(2,1)S(1)}, u32[]{:S(2)}, u32[]{:S(2)}) collective-permute-start(bf16[512,1,128]{2,0,1:T(8,128)(2,1)} %get-tuple-element.10), channel_id=1, source_target_pairs={{0,24},{8,32},{16,40},{24,48},{32,56},{40,64},{48,72},{56,80},{64,... | collective-permute-start | bytes 393224 | tf_op jit(solution)/shard_map/ppermute | solution.py:33
  494.3 9.1 %collective-permute-start.11 = (bf16[512,1,128]{2,0,1:T(8,128)(2,1)}, bf16[512,1,128]{2,0,1:T(8,128)(2,1)S(1)}, u32[]{:S(2)}, u32[]{:S(2)}) collective-permute-start(bf16[512,1,128]{2,0,1:T(8,128)(2,1)} %get-tuple-element.10), channel_id=1, source_target_pairs={{0,32},{8,40},{16,48},{24,56},{32,64},{40,72},{48,80},{56,88},{64,... | collective-permute-start | bytes 393224 | tf_op jit(solution)/shard_map/ppermute | solution.py:33
  498.2 18.6 %collective-permute-start.3 = (bf16[512,1,128]{2,0,1:T(8,128)(2,1)}, bf16[512,1,128]{2,0,1:T(8,128)(2,1)S(1)}, u32[]{:S(2)}, u32[]{:S(2)}) collective-permute-start(bf16[512,1,128]{2,0,1:T(8,128)(2,1)} %get-tuple-element.6), channel_id=1, source_target_pairs={{0,32},{8,40},{16,48},{24,56},{32,64},{40,72},{48,80},{56,88},{64,... | collective-permute-start | bytes 393224 | tf_op jit(solution)/shard_map/ppermute | solution.py:33
  504.1 12.6 %copy-start.3 = (bf16[2560,1,128]{2,0,1:T(8,128)(2,1)S(1)}, bf16[2560,1,128]{2,0,1:T(8,128)(2,1)}, u32[]{:S(2)}) copy-start(bf16[2560,1,128]{2,0,1:T(8,128)(2,1)} %get-tuple-element.5) | copy-start | bytes 1966084
  (8 other events, 31.1 us)
Sparse Core Ops, SparseCore 0:
  9.1 100.2 all-gather.2
  111.2 134.8 all-gather.4
  309.6 148.6 reduce-scatter.1
where the time goes:
time: 534 us; the launch traced here: 533 us
  waiting for transfers between devices  262 us (49%)
  blocking collectives  123 us (23%)
  starting transfers between devices  54.4 us (10%)
  matrix products  40.8 us (8%)
  other arithmetic  21.9 us (4%)
  local copies, waits for them, and re-layouts  16.3 us (3%)
  between operations  14.4 us (3%)
    reduce_scatter x1, waiting for transfers between devices, on_device(): lax.psum_scatter(partial_value.astype(jnp.bfloat16), 'wt', scatter_dimens...  132 us
    all_to_all x1, waiting for transfers between devices, summed_on_arrival(): lax.all_to_all(parts, axis, split_axis=0, concat_axis=0, tiled=True)  74.6 us
    all_gather x1, blocking collectives, on_device(): lax.all_gather(llm_scales, 'ctx', axis=2, tiled=True)  54.9 us
    all_gather x1, waiting for transfers between devices, merge_project(): codes_piece = lax.all_gather(merger_codes, 'ctx', axis=2, tiled=True)  47.2 us
    all_gather x1, blocking collectives, merge_project(): scale_piece = lax.all_gather(merger_scales, 'ctx', axis=2, tiled=True)  45.9 us
    ppermute x12, starting transfers between devices, passed_along(): lax.ppermute(value, axis, [(source, source + steps) for source in range(l...  37.9 us
    psum x1, blocking collectives, on_device(): squares = lax.psum(jnp.sum(values * values, axis=1), 'wt')  22.5 us
    sub x2, matrix products, softmax_rows(): raised = jnp.exp(masked - highest)  13.6 us
  transfers between devices with their start and end apart: 18, of which 4 were waited for; matrix products, arithmetic and copies ran while one was open for 10% of the time, Pallas kernels for 0%

commit v1 on v0

--- a/solution.py
+++ b/solution.py
@@ -154,7 +154,9 @@
 ):
     early_codes, early_scales = (
         lax.all_gather(llm_codes, "ctx", axis=2, tiled=True),
-        lax.all_gather(llm_scales, "ctx", axis=2, tiled=True),
+        jnp.concatenate(
+            lax.all_to_all(jnp.stack([llm_scales] * lax.axis_size("ctx")), "ctx", 0, 0), axis=2
+        ),
     )
     row_count = text_embed.shape[0]
     first = lax.axis_index("ctx") * row_count

time: 534 us -> 509 us (0.953)
  blocking collectives: 123 us -> 70.1 us
  waiting for transfers between devices: 262 us -> 280 us
  starting transfers between devices: 54.4 us -> 64.5 us
    all_gather x1 -> x0, blocking collectives: 54.9 us -> none  [on_device(): lax.all_gather(llm_scales, 'ctx', axis=2, tiled=True)]
    all_to_all x1, waiting for transfers between devices: 0.01 us -> 15.9 us  [route_tokens(): lax.all_to_all(packed, 'ctx', split_axis=0, concat_axis=0, tiled=True)]
    all_to_all x0 -> x1, waiting for transfers between devices: none -> 7.87 us  [on_device(): lax.all_to_all(jnp.stack([llm_scales] * lax.axis_size('ctx')), 'ctx', 0, 0)]
    reduce_scatter x1, waiting for transfers between devices: 132 us -> 126 us  [on_device(): lax.psum_scatter(partial_value.astype(jnp.bfloat16), 'wt', scatter_dimens...]
    ppermute x12, starting transfers between devices: 37.9 us -> 44.3 us  [passed_along(): lax.ppermute(value, axis, [(source, source + steps) for source in range(l...]
  transfers between devices with their start and end apart: 18 -> 19, of which waited for: 4 -> 6; matrix products, arithmetic and copies ran while one was open for 10% -> 11% of each run, Pallas kernels for 0% -> 0%
where the time goes in v1:
time: 509 us; the launch traced here: 508 us
  waiting for transfers between devices  280 us (55%)
  blocking collectives  70.1 us (14%)
  starting transfers between devices  64.5 us (13%)
  matrix products  40.8 us (8%)
  other arithmetic  21.5 us (4%)
  local copies, waits for them, and re-layouts  16.9 us (3%)
  between operations  14.4 us (3%)
    reduce_scatter x1, waiting for transfers between devices, on_device(): lax.psum_scatter(partial_value.astype(jnp.bfloat16), 'wt', scatter_dimens...  126 us
    all_to_all x1, waiting for transfers between devices, summed_on_arrival(): lax.all_to_all(parts, axis, split_axis=0, concat_axis=0, tiled=True)  74.6 us
    all_gather x1, waiting for transfers between devices, merge_project(): codes_piece = lax.all_gather(merger_codes, 'ctx', axis=2, tiled=True)  47.2 us
    all_gather x1, blocking collectives, merge_project(): scale_piece = lax.all_gather(merger_scales, 'ctx', axis=2, tiled=True)  45.9 us
    ppermute x12, starting transfers between devices, passed_along(): lax.ppermute(value, axis, [(source, source + steps) for source in range(l...  44.3 us
    psum x1, blocking collectives, on_device(): squares = lax.psum(jnp.sum(values * values, axis=1), 'wt')  24.2 us
    all_to_all x1, waiting for transfers between devices, route_tokens(): lax.all_to_all(packed, 'ctx', split_axis=0, concat_axis=0, tiled=True)  15.9 us
    sub x2, matrix products, softmax_rows(): raised = jnp.exp(masked - highest)  13.6 us
  transfers between devices with their start and end apart: 19, of which 6 were waited for; matrix products, arithmetic and copies ran while one was open for 11% of the time, Pallas kernels for 0%

profile of v1, /device:TPU:1, one launch (start us, length us, event | category | flops | bytes accessed | tf_op | source)
XLA Modules:
  0.0 508.3 jit_solution(10059325627666861314)
XLA Ops:
  16.2 45.9 %all_gather.10 = bf16[1,1,8192]{2,1,0:T(2,128)(2,1)S(1)} all-gather(bf16[1,1,256]{2,1,0:T(2,128)(2,1)S(1)} %copy-done.8), channel_id=1, replica_groups=mesh['ctx'=32,'wt'=8] {'ctx'}, dimensions={2}, use_global_device_ids=true | all-gather | bytes 16896 | tf_op jit(solution)/shard_map/all_gather | solution.py:97
  62.2 47.2 %all-gather.3.cloned.1.call-done = bf16[4,160,8192]{2,1,0:T(8,128)(2,1)} async-done(((bf16[4,160,256]{2,1,0:T(8,128)(2,1)}), bf16[4,160,8192]{2,1,0:T(8,128)(2,1)}) %all-gather.3.cloned.1.call-update) | async-done | bytes 10485776 | tf_op jit(solution)/shard_map/all_gather | solution.py:96
  109.4 6.2 %multiply_convert_fusion.1 = bf16[4,160,8192]{2,1,0:T(8,128)(2,1)S(1)} fusion(bf16[4,160,8192]{2,1,0:T(8,128)(2,1)} %all-gather.3.cloned.1.call-done, f32[8192]{0:T(1024)S(1)} %bitcast.113), kind=kLoop, calls=%fused_computation.6 | loop fusion | flops 15728640 | bytes 21004288 | tf_op jit(solution)/shard_map/convert_element_type | solution.py:99
  119.1 7.4 %all-to-all-start.1 = ((bf16[8,128,1024]{2,1,0:T(8,128)(2,1)}), bf16[8,128,1024]{2,1,0:T(8,128)(2,1)S(1)}, u32[]{:S(2)}, u32[]{:S(2)}) async-start(bf16[8,128,1024]{2,1,0:T(8,128)(2,1)} %bitcast.106), calls=%async_computation.1 | async-start | bytes 4194304 | tf_op jit(solution)/shard_map/all_to_all | solution.py:26
  127.6 74.6 %all-to-all-done.1 = bf16[8,128,1024]{2,1,0:T(8,128)(2,1)S(1)} async-done(((bf16[8,128,1024]{2,1,0:T(8,128)(2,1)}), bf16[8,128,1024]{2,1,0:T(8,128)(2,1)S(1)}, u32[]{:S(2)}, u32[]{:S(2)}) %all-to-all-start.1) | async-done | bytes 2097184 | tf_op jit(solution)/shard_map/all_to_all | solution.py:26
  202.2 4.9 all-to-all-start
  207.5 7.1 %all-to-all-done = s32[32,8,1]{1,2,0:T(1,128)S(1)} async-done(((s32[32,8,1]{1,2,0:T(1,128)}), s32[32,8,1]{1,2,0:T(1,128)S(1)}, u32[]{:S(2)}, u32[]{:S(2)}) %all-to-all-start) | async-done | bytes 1056 | tf_op jit(solution)/shard_map/all_to_all | solution.py:123
  215.2 4.0 all-to-all-start.3
  220.3 7.9 %all-to-all-done.3 = bf16[32,1,8,24]{3,2,1,0:T(8,128)(2,1)S(1)} async-done(((bf16[32,1,8,24]{3,2,1,0:T(8,128)(2,1)}), bf16[32,1,8,24]{3,2,1,0:T(8,128)(2,1)S(1)}, u32[]{:S(2)}, u32[]{:S(2)}) %all-to-all-start.3) | async-done | bytes 12320 | tf_op jit(solution)/shard_map/all_to_all | solution.py:158
  228.2 3.7 all-to-all-start.2
  232.4 15.9 %all-to-all-done.2 = bf16[32,8,1024]{2,1,0:T(8,128)(2,1)S(1)} async-done(((bf16[32,8,1024]{2,1,0:T(8,128)(2,1)}), bf16[32,8,1024]{2,1,0:T(8,128)(2,1)S(1)}, u32[]{:S(2)}, u32[]{:S(2)}) %all-to-all-start.2) | async-done | bytes 524320 | tf_op jit(solution)/shard_map/all_to_all | solution.py:122
  248.9 24.2 %psum.7 = f32[512]{0:T(512)S(1)} all-reduce(f32[512]{0:T(512)S(1)} %get-tuple-element.24), channel_id=1, replica_groups=mesh['ctx'=32,'wt'=8] {'wt'}, use_global_device_ids=true, to_apply=%region_8.9 | all-reduce | flops 512 | bytes 4096 | tf_op jit(solution)/shard_map/psum | solution.py:174
  273.1 11.6 %fusion.11 = bf16[512,8,768]{2,0,1:T(8,128)(2,1)} fusion(bf16[1024,8,768]{0,2,1:T(8,128)(2,1)} %all-gather.5.cloned.1.call-done, f32[8,768]{1,0:T(8,128)S(1)} %reshape.482, bf16[512,1024]{1,0:T(8,128)(2,1)S(1)} %get-tuple-element.25, f32[1024]{0:T(1024)S(1)} %copy-done.12, f32[512]{0:T(512)S(1)} %add_rsqrt_fusion), kind=kOutput, calls=%fused_computation.18 | convolution fusion | flops 6466568192 | bytes 19953664 | tf_op jit(solution)/shard_map/dot_general | solution.py:180
  285.4 7.1 %collective-permute-start.4 = (s32[512]{0:T(512)S(1)}, s32[512]{0:T(512)S(1)}, u32[]{:S(2)}, u32[]{:S(2)}) collective-permute-start(s32[512]{0:T(512)S(1)} %copy-done.4), channel_id=1, source_target_pairs={{0,8},{8,16},{16,24},{24,32},{32,40},{40,48},{48,56},{56,64},{64,7... | collective-permute-start | bytes 6152 | tf_op jit(solution)/shard_map/ppermute | solution.py:33
  294.2 3.4 collective-permute-start.6
  297.7 3.4 collective-permute-start.7
  304.2 3.5 and_and_fusion
  307.6 126.0 %reduce-scatter.2.cloned.1.call-done = bf16[512,1,768]{2,0,1:T(8,128)(2,1)} async-done(((bf16[512,8,768]{2,0,1:T(8,128)(2,1)}), bf16[512,1,768]{2,0,1:T(8,128)(2,1)}) %reduce-scatter.2.cloned.1.call-update) | async-done | bytes 786448 | tf_op jit(solution)/shard_map/reduce_scatter | solution.py:184
  436.9 5.7 %collective-permute-start = (bf16[512,1,128]{2,0,1:T(8,128)(2,1)}, bf16[512,1,128]{2,0,1:T(8,128)(2,1)S(1)}, u32[]{:S(2)}, u32[]{:S(2)}) collective-permute-start(bf16[512,1,128]{2,0,1:T(8,128)(2,1)} %get-tuple-element.6), channel_id=1, source_target_pairs={{0,8},{8,16},{16,24},{24,32},{32,40},{40,48},{48,56},{56,64},{64,7... | collective-permute-start | bytes 393224 | tf_op jit(solution)/shard_map/ppermute | solution.py:33
  445.8 3.4 collective-permute-start.2
  452.9 3.8 collective-permute-start.9
  473.6 4.5 collective-permute-start.3
  479.4 12.6 %fusion.83 = (f32[4,512]{1,0:T(4,128)S(1)}, f32[4,512,2560]{1,2,0:T(8,128)}) fusion(pred[512,2560]{0,1:T(8,128)(4,1)S(1)} %copy-done.2, bf16[2560,1,128]{2,0,1:T(8,128)(2,1)} %constant_dynamic-update-slice_fusion.7, bf16[512,4,128]{2,1,0:T(4,128)(2,1)S(1)} %convert_element_type.149), kind=kOutput, calls=%fused_computation.138 | convolution fusion | flops 1363151360 | bytes 23470080 | tf_op jit(solution)/shard_map/sub | solution.py:39
  492.2 8.5 %fusion.28 = bf16[128,4,512]{2,0,1:T(8,128)(2,1)S(1)} fusion(f32[4,512,2560]{1,2,0:T(8,128)} %get-tuple-element.27, f32[4,512]{1,0:T(4,128)S(1)} %get-tuple-element.26, bf16[2560,1,128]{2,0,1:T(8,128)(2,1)S(1)} %constant_dynamic-update-slice_fusion), kind=kOutput, calls=%fused_computation.44 | convolution fusion | flops 1352925184 | bytes 22159360 | tf_op jit(solution)/shard_map/jqk,kd->qjd/dot_general | solution.py:215
  (120 shorter events, 51.3 us)
Async XLA Ops:
  6.5 102.9 %all-gather.3.cloned.1.call-start = ((), (), s32[]{:S(2)}) async-start(), calls=%async_computation.5 | async-start | bytes 10813440 | tf_op jit(solution)/shard_map/all_gather | solution.py:96
  7.3 265.8 %all-gather.5.cloned.1.call-start = ((), (), s32[]{:S(2)}) async-start(), calls=%async_computation.6 | async-start | bytes 12976128 | tf_op jit(solution)/shard_map/all_gather | solution.py:156
  119.1 83.1 %all-to-all-start.1 = ((bf16[8,128,1024]{2,1,0:T(8,128)(2,1)}), bf16[8,128,1024]{2,1,0:T(8,128)(2,1)S(1)}, u32[]{:S(2)}, u32[]{:S(2)}) async-start(bf16[8,128,1024]{2,1,0:T(8,128)(2,1)} %bitcast.106), calls=%async_computation.1 | async-start | bytes 4194304 | tf_op jit(solution)/shard_map/all_to_all | solution.py:26
  126.5 88.0 %copy-start.7 = (bf16[1,8,24]{2,1,0:T(8,128)(2,1)S(1)}, bf16[1,8,24]{2,1,0:T(8,128)(2,1)}, u32[]{:S(2)}) copy-start(bf16[1,8,24]{2,1,0:T(8,128)(2,1)} %param.29) | copy-start | bytes 1156
  126.5 92.7 %copy-start.5 = (f32[1024]{0:T(1024)S(1)}, f32[1024]{0:T(1024)}, u32[]{:S(2)}) copy-start(f32[1024]{0:T(1024)} %param.24) | copy-start | bytes 12292
  202.2 12.4 %all-to-all-start = ((s32[32,8,1]{1,2,0:T(1,128)}), s32[32,8,1]{1,2,0:T(1,128)S(1)}, u32[]{:S(2)}, u32[]{:S(2)}) async-start(s32[32,8,1]{1,2,0:T(1,128)} %bitcast), calls=%async_computation | async-start | bytes 32768 | tf_op jit(solution)/shard_map/all_to_all | solution.py:123
  207.5 40.8 %copy-start.9 = (bf16[512,1024]{1,0:T(8,128)(2,1)S(1)}, bf16[512,1024]{1,0:T(8,128)(2,1)}, u32[]{:S(2)}) copy-start(bf16[512,1024]{1,0:T(8,128)(2,1)} %param.26) | copy-start | bytes 3145732
  215.2 13.0 %all-to-all-start.3 = ((bf16[32,1,8,24]{3,2,1,0:T(8,128)(2,1)}), bf16[32,1,8,24]{3,2,1,0:T(8,128)(2,1)S(1)}, u32[]{:S(2)}, u32[]{:S(2)}) async-start(bf16[32,1,8,24]{3,2,1,0:T(8,128)(2,1)} %stack.2), calls=%async_computation.3 | async-start | bytes 131072 | tf_op jit(solution)/shard_map/all_to_all | solution.py:158
  228.2 20.1 %all-to-all-start.2 = ((bf16[32,8,1024]{2,1,0:T(8,128)(2,1)}), bf16[32,8,1024]{2,1,0:T(8,128)(2,1)S(1)}, u32[]{:S(2)}, u32[]{:S(2)}) async-start(bf16[32,8,1024]{2,1,0:T(8,128)(2,1)} %fusion.32), calls=%async_computation.2 | async-start | bytes 1048576 | tf_op jit(solution)/shard_map/all_to_all | solution.py:122
  231.9 201.7 %reduce-scatter.2.cloned.1.call-start = ((), (), s32[]{:S(2)}) async-start(), calls=%async_computation.7 | async-start | bytes 7077888 | tf_op jit(solution)/shard_map/reduce_scatter | solution.py:184
  232.2 40.9 %copy-start.12 = (f32[1024]{0:T(1024)S(1)}, f32[1024]{0:T(1024)}, u32[]{:S(2)}) copy-start(f32[1024]{0:T(1024)} %param.27) | copy-start | bytes 12292
  285.4 18.7 %collective-permute-start.4 = (s32[512]{0:T(512)S(1)}, s32[512]{0:T(512)S(1)}, u32[]{:S(2)}, u32[]{:S(2)}) collective-permute-start(s32[512]{0:T(512)S(1)} %copy-done.4), channel_id=1, source_target_pairs={{0,8},{8,16},{16,24},{24,32},{32,40},{40,48},{48,56},{56,64},{64,7... | collective-permute-start | bytes 6152 | tf_op jit(solution)/shard_map/ppermute | solution.py:33
  292.6 11.6 %collective-permute-start.5 = (s32[512]{0:T(512)S(1)}, s32[512]{0:T(512)S(1)}, u32[]{:S(2)}, u32[]{:S(2)}) collective-permute-start(s32[512]{0:T(512)S(1)} %copy-done.4), channel_id=1, source_target_pairs={{0,16},{8,24},{16,32},{24,40},{32,48},{40,56},{48,64},{56,72},{64,... | collective-permute-start | bytes 6152 | tf_op jit(solution)/shard_map/ppermute | solution.py:33
  294.2 9.9 %collective-permute-start.6 = (s32[512]{0:T(512)S(1)}, s32[512]{0:T(512)S(1)}, u32[]{:S(2)}, u32[]{:S(2)}) collective-permute-start(s32[512]{0:T(512)S(1)} %copy-done.4), channel_id=1, source_target_pairs={{0,24},{8,32},{16,40},{24,48},{32,56},{40,64},{48,72},{56,80},{64,... | collective-permute-start | bytes 6152 | tf_op jit(solution)/shard_map/ppermute | solution.py:33
  297.7 6.5 %collective-permute-start.7 = (s32[512]{0:T(512)S(1)}, s32[512]{0:T(512)S(1)}, u32[]{:S(2)}, u32[]{:S(2)}) collective-permute-start(s32[512]{0:T(512)S(1)} %copy-done.4), channel_id=1, source_target_pairs={{0,32},{8,40},{16,48},{24,56},{32,64},{40,72},{48,80},{56,88},{64,... | collective-permute-start | bytes 6152 | tf_op jit(solution)/shard_map/ppermute | solution.py:33
  436.9 55.1 %collective-permute-start = (bf16[512,1,128]{2,0,1:T(8,128)(2,1)}, bf16[512,1,128]{2,0,1:T(8,128)(2,1)S(1)}, u32[]{:S(2)}, u32[]{:S(2)}) collective-permute-start(bf16[512,1,128]{2,0,1:T(8,128)(2,1)} %get-tuple-element.6), channel_id=1, source_target_pairs={{0,8},{8,16},{16,24},{24,32},{32,40},{40,48},{48,56},{56,64},{64,7... | collective-permute-start | bytes 393224 | tf_op jit(solution)/shard_map/ppermute | solution.py:33
  442.6 49.4 %collective-permute-start.1 = (bf16[512,1,128]{2,0,1:T(8,128)(2,1)}, bf16[512,1,128]{2,0,1:T(8,128)(2,1)S(1)}, u32[]{:S(2)}, u32[]{:S(2)}) collective-permute-start(bf16[512,1,128]{2,0,1:T(8,128)(2,1)} %get-tuple-element.6), channel_id=1, source_target_pairs={{0,16},{8,24},{16,32},{24,40},{32,48},{40,56},{48,64},{56,72},{64,... | collective-permute-start | bytes 393224 | tf_op jit(solution)/shard_map/ppermute | solution.py:33
  445.8 46.4 %collective-permute-start.2 = (bf16[512,1,128]{2,0,1:T(8,128)(2,1)}, bf16[512,1,128]{2,0,1:T(8,128)(2,1)S(1)}, u32[]{:S(2)}, u32[]{:S(2)}) collective-permute-start(bf16[512,1,128]{2,0,1:T(8,128)(2,1)} %get-tuple-element.6), channel_id=1, source_target_pairs={{0,24},{8,32},{16,40},{24,48},{32,56},{40,64},{48,72},{56,80},{64,... | collective-permute-start | bytes 393224 | tf_op jit(solution)/shard_map/ppermute | solution.py:33
  450.3 14.4 %collective-permute-start.8 = (bf16[512,1,128]{2,0,1:T(8,128)(2,1)}, bf16[512,1,128]{2,0,1:T(8,128)(2,1)}, u32[]{:S(2)}, u32[]{:S(2)}) collective-permute-start(bf16[512,1,128]{2,0,1:T(8,128)(2,1)} %get-tuple-element.10), channel_id=1, source_target_pairs={{0,8},{8,16},{16,24},{24,32},{32,40},{40,48},{48,56},{56,64},{64,7... | collective-permute-start | bytes 393224 | tf_op jit(solution)/shard_map/ppermute | solution.py:33
  452.9 16.7 %collective-permute-start.9 = (bf16[512,1,128]{2,0,1:T(8,128)(2,1)}, bf16[512,1,128]{2,0,1:T(8,128)(2,1)}, u32[]{:S(2)}, u32[]{:S(2)}) collective-permute-start(bf16[512,1,128]{2,0,1:T(8,128)(2,1)} %get-tuple-element.10), channel_id=1, source_target_pairs={{0,16},{8,24},{16,32},{24,40},{32,48},{40,56},{48,64},{56,72},{64,... | collective-permute-start | bytes 393224 | tf_op jit(solution)/shard_map/ppermute | solution.py:33
  464.6 14.8 %copy-start.2 = (pred[512,2560]{0,1:T(8,128)(4,1)S(1)}, pred[512,2560]{0,1:T(8,128)(4,1)}, u32[]{:S(2)}) copy-start(pred[512,2560]{0,1:T(8,128)(4,1)} %and_and_fusion) | copy-start | bytes 3932164
  464.7 8.8 %collective-permute-start.10 = (bf16[512,1,128]{2,0,1:T(8,128)(2,1)}, bf16[512,1,128]{2,0,1:T(8,128)(2,1)S(1)}, u32[]{:S(2)}, u32[]{:S(2)}) collective-permute-start(bf16[512,1,128]{2,0,1:T(8,128)(2,1)} %get-tuple-element.10), channel_id=1, source_target_pairs={{0,24},{8,32},{16,40},{24,48},{32,56},{40,64},{48,72},{56,80},{64,... | collective-permute-start | bytes 393224 | tf_op jit(solution)/shard_map/ppermute | solution.py:33
  469.6 9.2 %collective-permute-start.11 = (bf16[512,1,128]{2,0,1:T(8,128)(2,1)}, bf16[512,1,128]{2,0,1:T(8,128)(2,1)S(1)}, u32[]{:S(2)}, u32[]{:S(2)}) collective-permute-start(bf16[512,1,128]{2,0,1:T(8,128)(2,1)} %get-tuple-element.10), channel_id=1, source_target_pairs={{0,32},{8,40},{16,48},{24,56},{32,64},{40,72},{48,80},{56,88},{64,... | collective-permute-start | bytes 393224 | tf_op jit(solution)/shard_map/ppermute | solution.py:33
  473.6 18.6 %collective-permute-start.3 = (bf16[512,1,128]{2,0,1:T(8,128)(2,1)}, bf16[512,1,128]{2,0,1:T(8,128)(2,1)S(1)}, u32[]{:S(2)}, u32[]{:S(2)}) collective-permute-start(bf16[512,1,128]{2,0,1:T(8,128)(2,1)} %get-tuple-element.6), channel_id=1, source_target_pairs={{0,32},{8,40},{16,48},{24,56},{32,64},{40,72},{48,80},{56,88},{64,... | collective-permute-start | bytes 393224 | tf_op jit(solution)/shard_map/ppermute | solution.py:33
  (9 other events, 43.7 us)
Sparse Core Ops, SparseCore 0:
  9.1 100.2 all-gather.2
  111.2 124.3 all-gather.4
  284.9 148.6 reduce-scatter.1
